TPU v7x, 256 devices: a whole 4x4x8 slice. The times are simulated.
256 devices in a mesh: expert: 16 (over x, y), context: 8 (over z_hi, core), dp: 2 (over z_lo).
Axes of the slice: x: 4, y: 4, z: 8 (z_hi: 4, z_lo: 2; z = z_hi * 2 + z_lo), core: 2. Of those that a mesh axis runs over, the one named last changes fastest.
Arguments:
- tokens: bfloat16 [32768, 2048], P(('expert', 'context', 'dp')), may hold values from -6 to 6
- routes: int32 [32768, 2], P(('expert', 'context', 'dp')), may hold values from 0 to 127, all different within a row; in each aligned block of 128 rows (0 to 127, 128 to 255, ...) at most 4 rows name the same one
- gates: float32 [32768, 2], P(('expert', 'context', 'dp')), may hold values from 0.3 to 0.9
- out_grad: bfloat16 [32768, 2048], P(('expert', 'context', 'dp')), may hold values from -6 to 6
- w_gate: bfloat16 [128, 2048, 768], P(('expert', 'context'), 'dp'), may hold values from -0.125 to 0.125
- w_up: bfloat16 [128, 2048, 768], P(('expert', 'context'), 'dp'), may hold values from -0.125 to 0.125
- w_down: bfloat16 [128, 2048, 768], P(('expert', 'context'), 'dp'), may hold values from -0.21875 to 0.21875
Outputs:
- mixed: bfloat16 [32768, 2048], P(('expert', 'context', 'dp'))
- token_grad: bfloat16 [32768, 2048], P(('expert', 'context', 'dp'))
- gate_grad: float32 [32768, 2], P(('expert', 'context', 'dp'))
- w_gate_grad: bfloat16 [128, 2048, 768], P(('expert', 'context'), 'dp')
- w_up_grad: bfloat16 [128, 2048, 768], P(('expert', 'context'), 'dp')
- w_down_grad: bfloat16 [128, 2048, 768], P(('expert', 'context'), 'dp')
Inputs may be any that keep to these rules, and one draw needn't show every extreme that they name: `routes`: each row names 2 different experts; in each aligned block of 128 rows (the rows of one device) no expert is named by more than 4 rows, a bound that some block reaches.
All inputs are finite; a program needn't handle non-finite values.
Results may differ from a plain program's by a relative error of at most 0.0065.
Values may be sent and summed in bfloat16 or wider, within the bound.
A program may use at most 128 MiB of HBM per device.

v0:
```python
import jax
import jax.numpy as jnp
from jax import lax
from jax.sharding import PartitionSpec as P


def contract(left, right, left_dim, right_dim):
    return lax.dot_general(
        left, right, (((left_dim,), (right_dim,)), ((), ())), preferred_element_type=jnp.float32
    )


def expert_block(rows_x, rows_dy, gate_w, up_w, down_w):
    gate_pre = contract(rows_x, gate_w, 1, 0)
    up_pre = contract(rows_x, up_w, 1, 0)
    sig_gate = jax.nn.sigmoid(gate_pre)
    active = gate_pre * sig_gate
    slope = sig_gate * (1.0 + gate_pre * (1.0 - sig_gate))
    hidden = (active * up_pre).astype(jnp.bfloat16)
    expert_out = contract(hidden, down_w, 1, 1).astype(jnp.bfloat16)
    hidden_grad = contract(rows_dy, down_w, 1, 0)
    grad_gate = (hidden_grad * up_pre * slope).astype(jnp.bfloat16)
    grad_up = (hidden_grad * active).astype(jnp.bfloat16)
    expert_dx = (contract(grad_gate, gate_w, 1, 1) + contract(grad_up, up_w, 1, 1)).astype(
        jnp.bfloat16
    )
    return (expert_out, expert_dx, hidden, grad_gate, grad_up)


def shards(tokens, routes, gates, out_grad, w_gate, w_up, w_down):
    experts = lax.axis_size(("expert", "context"))
    local_tokens, top_count = routes.shape
    model_width = tokens.shape[1]
    slot_total = local_tokens * top_count
    capacity = max(2, 2 * slot_total // experts)
    slot_expert = routes.reshape(-1)
    one_hot = (slot_expert[:, None] == jnp.arange(experts, dtype=jnp.int32)[None, :]).astype(
        jnp.int32
    )
    before = jnp.cumsum(one_hot, axis=0) - one_hot
    slot_place = jnp.sum(before * one_hot, axis=1)
    slot_index = slot_expert * capacity + slot_place
    owner_slot = (
        jnp.zeros((experts * capacity,), jnp.int32)
        .at[slot_index]
        .set(jnp.arange(slot_total, dtype=jnp.int32))
    )
    filled = jnp.zeros((experts * capacity,), jnp.bool_).at[slot_index].set(True)
    token_of = owner_slot // top_count
    send_rows = jnp.where(filled[:, None], tokens[token_of], jnp.zeros((), tokens.dtype))
    gate_of = jnp.where(filled, gates.reshape(-1)[owner_slot], 0.0)
    send_grads = (gate_of[:, None] * out_grad[token_of].astype(jnp.float32)).astype(jnp.bfloat16)
    gate_full, up_full, down_full = (
        lax.all_gather(w_gate, "dp", axis=1, tiled=True),
        lax.all_gather(w_up, "dp", axis=1, tiled=True),
        lax.all_gather(w_down, "dp", axis=1, tiled=True),
    )
    block_shape = (experts, capacity, model_width)
    recv_rows, recv_grads = (
        lax.all_to_all(
            send_rows.reshape(block_shape),
            ("expert", "context"),
            split_axis=0,
            concat_axis=1,
            tiled=True,
        ),
        lax.all_to_all(
            send_grads.reshape(block_shape),
            ("expert", "context"),
            split_axis=0,
            concat_axis=1,
            tiled=True,
        ),
    )
    rows_x = recv_rows.reshape(-1, model_width)
    rows_dy = recv_grads.reshape(-1, model_width)
    expert_out, expert_dx, hidden, grad_gate, grad_up = expert_block(
        rows_x, rows_dy, gate_full[0], up_full[0], down_full[0]
    )
    back_out, back_dx = (
        lax.all_to_all(
            expert_out[None], ("expert", "context"), split_axis=1, concat_axis=0, tiled=True
        ),
        lax.all_to_all(
            expert_dx[None], ("expert", "context"), split_axis=1, concat_axis=0, tiled=True
        ),
    )
    token_shape = (local_tokens, top_count, model_width)
    out_rows = back_out.reshape(-1, model_width)[slot_index].reshape(token_shape)
    dx_rows = back_dx.reshape(-1, model_width)[slot_index].reshape(token_shape)
    mixed = jnp.sum(gates[:, :, None] * out_rows.astype(jnp.float32), axis=1).astype(jnp.bfloat16)
    token_grad = jnp.sum(dx_rows.astype(jnp.float32), axis=1).astype(jnp.bfloat16)
    gate_grad = jnp.sum(
        out_rows.astype(jnp.float32) * out_grad[:, None, :].astype(jnp.float32), axis=2
    )
    ff_width = hidden.shape[1]
    summed = lax.psum_scatter(
        jnp.concatenate(
            [
                contract(rows_x, grad_gate, 0, 0),
                contract(rows_x, grad_up, 0, 0),
                contract(rows_dy, hidden, 0, 0),
            ],
            axis=1,
        ),
        "dp",
        scatter_dimension=0,
        tiled=True,
    )
    w_gate_grad = summed[:, :ff_width].astype(jnp.bfloat16)[None]
    w_up_grad = summed[:, ff_width : 2 * ff_width].astype(jnp.bfloat16)[None]
    w_down_grad = summed[:, 2 * ff_width :].astype(jnp.bfloat16)[None]
    return (mixed, token_grad, gate_grad, w_gate_grad, w_up_grad, w_down_grad)


def solution(mesh):
    in_specs = (
        P(("expert", "context", "dp"), None),
        P(("expert", "context", "dp"), None),
        P(("expert", "context", "dp"), None),
        P(("expert", "context", "dp"), None),
        P(("expert", "context"), "dp", None),
        P(("expert", "context"), "dp", None),
        P(("expert", "context"), "dp", None),
    )
    out_specs = (
        P(("expert", "context", "dp"), None),
        P(("expert", "context", "dp"), None),
        P(("expert", "context", "dp"), None),
        P(("expert", "context"), "dp", None),
        P(("expert", "context"), "dp", None),
        P(("expert", "context"), "dp", None),
    )
    return jax.shard_map(shards, mesh=mesh, in_specs=in_specs, out_specs=out_specs, check_vma=False)
```

profile of v0, /device:TPU:1, one launch (start us, length us, event | category | flops | bytes accessed | tf_op | source)
XLA Modules:
  0.0 601.9 jit_solution(1598970839343315732)
XLA Ops:
  18.3 3.9 broadcast_select_fusion
  22.2 17.0 %all-to-all-start = ((bf16[128,4,2048]{2,1,0:T(4,128)(2,1)}), bf16[128,4,2048]{2,1,0:T(4,128)(2,1)}, u32[]{:S(2)}, u32[]{:S(2)}) async-start(bf16[128,4,2048]{2,1,0:T(4,128)(2,1)} %broadcast_select_fusion), calls=%async_computation | async-start | bytes 4194304 | tf_op jit(solution)/shard_map/all_to_all | solution.py:60
  40.2 3.5 gather_fusion.2
  49.4 4.3 multiply_convert_fusion
  53.7 63.1 %all-to-all-done = bf16[128,4,2048]{2,1,0:T(4,128)(2,1)} async-done(((bf16[128,4,2048]{2,1,0:T(4,128)(2,1)}), bf16[128,4,2048]{2,1,0:T(4,128)(2,1)}, u32[]{:S(2)}, u32[]{:S(2)}) %all-to-all-start) | async-done | bytes 2097184 | tf_op jit(solution)/shard_map/all_to_all | solution.py:60
  116.8 7.0 %all-to-all-start.2 = ((bf16[128,4,2048]{2,1,0:T(4,128)(2,1)}), bf16[128,4,2048]{2,1,0:T(4,128)(2,1)}, u32[]{:S(2)}, u32[]{:S(2)}) async-start(bf16[128,4,2048]{2,1,0:T(4,128)(2,1)} %multiply_convert_fusion), calls=%async_computation.2 | async-start | bytes 4194304 | tf_op jit(solution)/shard_map/all_to_all | solution.py:67
  127.3 71.2 %all-to-all-done.2 = bf16[128,4,2048]{2,1,0:T(4,128)(2,1)} async-done(((bf16[128,4,2048]{2,1,0:T(4,128)(2,1)}), bf16[128,4,2048]{2,1,0:T(4,128)(2,1)}, u32[]{:S(2)}, u32[]{:S(2)}) %all-to-all-start.2) | async-done | bytes 2097184 | tf_op jit(solution)/shard_map/all_to_all | solution.py:67
  198.5 3.9 reshape.130
  202.5 4.8 fusion.6
  207.3 5.5 fusion
  212.8 43.3 %all-gather.4.cloned.1.call-done = bf16[1,2048,768]{2,1,0:T(8,128)(2,1)} async-done(((bf16[1,1024,768]{2,1,0:T(8,128)(2,1)}), bf16[1,2048,768]{2,1,0:T(8,128)(2,1)}) %all-gather.4.cloned.1.call-update) | async-done | bytes 3145744 | tf_op jit(solution)/shard_map/all_gather | solution.py:54
  256.0 5.3 multiply_convert_fusion.2
  267.1 7.2 %pad_maximum_fusion = f32[2048,2304]{0,1:T(8,128)} fusion(f32[2048,768]{0,1:T(8,128)S(1)} %fusion.37, f32[2048,768]{0,1:T(8,128)S(1)} %fusion.36, f32[2048,768]{0,1:T(8,128)S(1)} %fusion.35), kind=kLoop, calls=%fused_computation.7 | loop fusion | flops 9437184 | bytes 37748736 | tf_op jit(solution)/shard_map/concatenate | solution.py:98
  275.5 3.9 fusion.4
  281.2 5.3 copy.61
  287.0 13.2 %reduce.6 = bf16[512,2048]{1,0:T(8,128)(2,1)S(1)} reduce(bf16[512,1,2048]{2,1,0:T(2,128)(2,1)} %bitcast.80, bf16[]{:T(256)} %broadcast.106), dimensions={1}, to_apply=%bitcast.71.reduce_sub_computation | reduce | bytes 4194306
  303.0 13.7 %all-to-all-start.3 = ((bf16[128,2,4096]{2,1,0:T(2,128)(2,1)}), bf16[128,2,4096]{2,1,0:T(2,128)(2,1)S(1)}, u32[]{:S(2)}, u32[]{:S(2)}) async-start(bf16[128,2,4096]{2,1,0:T(2,128)(2,1)} %reshape.200), calls=%async_computation.3 | async-start | bytes 4194304 | tf_op jit(solution)/shard_map/all_to_all | solution.py:84
  316.7 3.7 fusion.17
  320.4 5.3 copy.62
  325.7 14.4 %reduce.5 = bf16[512,2048]{1,0:T(8,128)(2,1)} reduce(bf16[512,1,2048]{2,1,0:T(2,128)(2,1)} %bitcast.81, bf16[]{:T(256)} %broadcast.106), dimensions={1}, to_apply=%bitcast.72.reduce_sub_computation | reduce | bytes 4194306
  340.2 4.5 reshape.198
  344.7 50.2 %all-to-all-done.3 = bf16[128,2,4096]{2,1,0:T(2,128)(2,1)S(1)} async-done(((bf16[128,2,4096]{2,1,0:T(2,128)(2,1)}), bf16[128,2,4096]{2,1,0:T(2,128)(2,1)S(1)}, u32[]{:S(2)}, u32[]{:S(2)}) %all-to-all-start.3) | async-done | bytes 2097184 | tf_op jit(solution)/shard_map/all_to_all | solution.py:84
  394.9 7.0 %all-to-all-start.1 = ((bf16[128,2,4096]{2,1,0:T(2,128)(2,1)}), bf16[128,2,4096]{2,1,0:T(2,128)(2,1)}, u32[]{:S(2)}, u32[]{:S(2)}) async-start(bf16[128,2,4096]{2,1,0:T(2,128)(2,1)} %reshape.198), calls=%async_computation.1 | async-start | bytes 4194304 | tf_op jit(solution)/shard_map/all_to_all | solution.py:81
  403.0 6.7 %reshape.201 = bf16[512,1,2048]{2,1,0:T(2,128)(2,1)} reshape(bf16[128,2,4096]{2,1,0:T(2,128)(2,1)S(1)} %all-to-all-done.3) | data formatting | bytes 4194304
  409.7 3.5 copy.59
  418.1 61.1 %all-to-all-done.1 = bf16[128,2,4096]{2,1,0:T(2,128)(2,1)} async-done(((bf16[128,2,4096]{2,1,0:T(2,128)(2,1)}), bf16[128,2,4096]{2,1,0:T(2,128)(2,1)}, u32[]{:S(2)}, u32[]{:S(2)}) %all-to-all-start.1) | async-done | bytes 2097184 | tf_op jit(solution)/shard_map/all_to_all | solution.py:81
  479.1 13.9 %reshape.199 = bf16[512,1,2048]{2,1,0:T(2,128)(2,1)} reshape(bf16[128,2,4096]{2,1,0:T(2,128)(2,1)} %all-to-all-done.1) | data formatting | bytes 4194304
  493.0 3.6 copy.60
  501.3 6.2 %multiply_reduce_fusion = (f32[128,2]{1,0:T(8,128)S(1)}, bf16[128,2048]{1,0:T(8,128)(2,1)}) fusion(f32[128,2,2048]{2,1,0:T(2,128)S(1)} %reshape.133, f32[128,2048]{1,0:T(8,128)} %convert_element_type.69, f32[128,2]{1,0:T(8,128)S(1)} %copy.40), kind=kLoop, calls=%fused_computation.27 | loop fusion | flops 1834752 | bytes 3672064 | tf_op jit(solution)/shard_map/reduce_sum | solution.py:93
  508.1 4.6 reduce_sum.44
  512.7 69.0 %reduce-scatter.2.cloned.1.call-done = f32[1024,2304]{0,1:T(8,128)} async-done(((f32[2048,2304]{0,1:T(8,128)}), f32[1024,2304]{0,1:T(8,128)}) %reduce-scatter.2.cloned.1.call-update) | async-done | bytes 9437200 | tf_op jit(solution)/shard_map/reduce_scatter | solution.py:97
  581.7 4.5 convert.8
  (79 shorter events, 53.4 us)
Async XLA Ops:
  7.2 6.5 %copy-start = (bf16[128,2048]{1,0:T(8,128)(2,1)S(1)}, bf16[128,2048]{1,0:T(8,128)(2,1)}, u32[]{:S(2)}) copy-start(bf16[128,2048]{1,0:T(8,128)(2,1)} %param.7) | copy-start | bytes 1572868
  7.2 195.3 %all-gather.6.cloned.1.call-start = ((), (), s32[]{:S(2)}) async-start(), calls=%async_computation.6 | async-start | bytes 4718592 | tf_op jit(solution)/shard_map/all_gather | solution.py:55
  22.2 17.8 %copy-start.8 = (f32[128,2]{0,1:T(2,128)S(1)}, f32[128,2]{0,1:T(2,128)}, u32[]{:S(2)}) copy-start(f32[128,2]{0,1:T(2,128)} %param.9) | copy-start | bytes 3076
  22.2 94.6 %all-to-all-start = ((bf16[128,4,2048]{2,1,0:T(4,128)(2,1)}), bf16[128,4,2048]{2,1,0:T(4,128)(2,1)}, u32[]{:S(2)}, u32[]{:S(2)}) async-start(bf16[128,4,2048]{2,1,0:T(4,128)(2,1)} %broadcast_select_fusion), calls=%async_computation | async-start | bytes 4194304 | tf_op jit(solution)/shard_map/all_to_all | solution.py:60
  39.2 4.7 copy-start.2
  39.2 168.1 %all-gather.8.cloned.1.call-start = ((), (), s32[]{:S(2)}) async-start(), calls=%async_computation.7 | async-start | bytes 4718592 | tf_op jit(solution)/shard_map/all_gather | solution.py:56
  116.8 81.7 %all-to-all-start.2 = ((bf16[128,4,2048]{2,1,0:T(4,128)(2,1)}), bf16[128,4,2048]{2,1,0:T(4,128)(2,1)}, u32[]{:S(2)}, u32[]{:S(2)}) async-start(bf16[128,4,2048]{2,1,0:T(4,128)(2,1)} %multiply_convert_fusion), calls=%async_computation.2 | async-start | bytes 4194304 | tf_op jit(solution)/shard_map/all_to_all | solution.py:67
  123.8 132.2 %all-gather.4.cloned.1.call-start = ((), (), s32[]{:S(2)}) async-start(), calls=%async_computation.5 | async-start | bytes 4718592 | tf_op jit(solution)/shard_map/all_gather | solution.py:54
  124.6 457.1 %reduce-scatter.2.cloned.1.call-start = ((), (), s32[]{:S(2)}) async-start(), calls=%async_computation.8 | async-start | bytes 28311552 | tf_op jit(solution)/shard_map/reduce_scatter | solution.py:97
  256.0 5.3 copy-start.3
  261.3 2.0 copy-start.4
  261.3 3.9 copy-start.6
  274.3 1.1 copy-start.7
  275.4 3.9 copy-start.5
  275.5 3.9 copy-start.9
  303.0 91.9 %all-to-all-start.3 = ((bf16[128,2,4096]{2,1,0:T(2,128)(2,1)}), bf16[128,2,4096]{2,1,0:T(2,128)(2,1)S(1)}, u32[]{:S(2)}, u32[]{:S(2)}) async-start(bf16[128,2,4096]{2,1,0:T(2,128)(2,1)} %reshape.200), calls=%async_computation.3 | async-start | bytes 4194304 | tf_op jit(solution)/shard_map/all_to_all | solution.py:84
  394.9 84.2 %all-to-all-start.1 = ((bf16[128,2,4096]{2,1,0:T(2,128)(2,1)}), bf16[128,2,4096]{2,1,0:T(2,128)(2,1)}, u32[]{:S(2)}, u32[]{:S(2)}) async-start(bf16[128,2,4096]{2,1,0:T(2,128)(2,1)} %reshape.198), calls=%async_computation.1 | async-start | bytes 4194304 | tf_op jit(solution)/shard_map/all_to_all | solution.py:81
  590.9 4.2 copy-start.1
Sparse Core Ops, SparseCore 0:
  9.8 98.2 all-gather.5
  109.9 93.1 all-gather.7
  205.0 51.0 all-gather.3
  274.5 307.1 reduce-scatter.1
where the time goes:
time: 612 us; the launch traced here: 602 us
  waiting for transfers between devices  360 us (59%)
  local copies, waits for them, and re-layouts  91.6 us (15%)
  other arithmetic  60.4 us (10%)
  starting transfers between devices  44.9 us (7%)
  matrix products  30.7 us (5%)
  between operations  14.4 us (2%)
    all_to_all x1, waiting for transfers between devices, shards(): lax.all_to_all(send_grads.reshape(block_shape), ('expert', 'context'), sp...  71.2 us
    reduce_scatter x1, waiting for transfers between devices, shards(): lax.psum_scatter(jnp.concatenate([contract(rows_x, grad_gate, 0, 0), cont...  69 us
    all_to_all x1, waiting for transfers between devices, shards(): lax.all_to_all(send_rows.reshape(block_shape), ('expert', 'context'), spl...  63.1 us
    all_to_all x1, waiting for transfers between devices, shards(): lax.all_to_all(expert_out[None], ('expert', 'context'), split_axis=1, con...  61.1 us
    all_to_all x1, waiting for transfers between devices, shards(): lax.all_to_all(expert_dx[None], ('expert', 'context'), split_axis=1, conc...  50.2 us
    unnamed x34, local copies, waits for them, and re-layouts  45 us
    all_gather x1, waiting for transfers between devices, shards(): lax.all_gather(w_gate, 'dp', axis=1, tiled=True)  43.3 us
    dot_general x9, matrix products, contract(): lax.dot_general(left, right, (((left_dim,), (right_dim,)), ((), ())), pre...  30.7 us
  transfers between devices with their start and end apart: 8, of which 6 were waited for; matrix products, arithmetic and copies ran while one was open for 25% of the time, Pallas kernels for 0%

commit v1 on v0

v1 whole, which is shorter than its diff:
```python
import jax
import jax.numpy as jnp
from jax import lax
from jax.sharding import PartitionSpec as P

PEERS = ("dp", "expert", "context")


def contract(left, right, left_dim, right_dim):
    return lax.dot_general(
        left, right, (((left_dim,), (right_dim,)), ((), ())), preferred_element_type=jnp.float32
    )


def shards(tokens, routes, gates, out_grad, w_gate, w_up, w_down):
    experts = lax.axis_size(("expert", "context"))
    halves = lax.axis_size("dp")
    devices = experts * halves
    local_tokens, top_count = routes.shape
    width = tokens.shape[1] // halves
    ff = w_gate.shape[2]
    capacity = max(2, 2 * local_tokens * top_count // experts)
    block = 2 * capacity

    slots = jnp.concatenate([routes[:, k] for k in range(top_count)])
    count = slots.shape[0]
    order = lax.broadcasted_iota(jnp.int32, (count, count), 0)
    before = lax.broadcasted_iota(jnp.int32, (count, count), 1) < order
    place = jnp.sum(((slots[:, None] == slots[None, :]) & before).astype(jnp.int32), axis=1)
    place = (slots * block + place).reshape(top_count, local_tokens)
    rows = lax.broadcasted_iota(jnp.int32, (experts * block, local_tokens), 0)
    hits_x = [rows == place[k][None, :] for k in range(top_count)]
    hits_dy = [rows == place[k][None, :] + capacity for k in range(top_count)]
    pick_x = sum(h.astype(jnp.bfloat16) for h in hits_x)
    pick_dy = sum(h.astype(jnp.bfloat16) for h in hits_dy)
    gate_of = sum(
        jnp.sum(jnp.where(h, gates[:, k][None, :], 0.0), axis=1) for k, h in enumerate(hits_dy)
    )

    def half(array, h):
        return array[:, h * width : (h + 1) * width]

    sends = []
    for h in range(halves):
        picked = contract(pick_x, half(tokens, h), 1, 0)
        graded = gate_of[:, None] * contract(pick_dy, half(out_grad, h), 1, 0)
        sends.append((picked + graded).astype(jnp.bfloat16))
    send = jnp.stack(sends).reshape(devices, block, width)
    recv = lax.all_to_all(send, PEERS, split_axis=0, concat_axis=0, tiled=True)
    rows_x = recv[:, :capacity].reshape(devices * capacity, width)
    rows_dy = recv[:, capacity:].reshape(devices * capacity, width)

    gate_w, up_w, down_w = w_gate[0], w_up[0], w_down[0]
    part_gate = contract(rows_x, gate_w, 1, 0)
    part_up = contract(rows_x, up_w, 1, 0)
    part_hidden = contract(rows_dy, down_w, 1, 0)
    swap = [(d, halves - 1 - d) for d in range(halves)]
    mine = jnp.concatenate(
        [p.astype(jnp.bfloat16) for p in (part_gate, part_up, part_hidden)], axis=1
    )
    other = lax.ppermute(mine, "dp", swap).astype(jnp.float32)
    gate_pre = part_gate + other[:, :ff]
    up_pre = part_up + other[:, ff : 2 * ff]
    hidden_grad = part_hidden + other[:, 2 * ff :]
    sig_gate = jax.nn.sigmoid(gate_pre)
    active = gate_pre * sig_gate
    slope = sig_gate * (1.0 + gate_pre * (1.0 - sig_gate))
    hidden = (active * up_pre).astype(jnp.bfloat16)
    grad_gate = (hidden_grad * up_pre * slope).astype(jnp.bfloat16)
    grad_up = (hidden_grad * active).astype(jnp.bfloat16)
    expert_out = contract(hidden, down_w, 1, 1).astype(jnp.bfloat16)
    expert_dx = (contract(grad_gate, gate_w, 1, 1) + contract(grad_up, up_w, 1, 1)).astype(
        jnp.bfloat16
    )
    back = jnp.concatenate(
        [
            expert_out.reshape(devices, capacity, width),
            expert_dx.reshape(devices, capacity, width),
        ],
        axis=1,
    )
    back = lax.all_to_all(back, PEERS, split_axis=0, concat_axis=0, tiled=True)
    back = back.reshape(halves, experts * block, width)
    mixed, token_grad, gate_grad = [], [], 0.0
    for h in range(halves):
        outs = [contract(x.astype(jnp.bfloat16), back[h], 0, 0) for x in hits_x]
        cot = half(out_grad, h).astype(jnp.float32)
        mixed.append(sum(gates[:, k][:, None] * out for k, out in enumerate(outs)))
        gate_grad += jnp.stack([jnp.sum(out * cot, axis=1) for out in outs], axis=1)
        token_grad.append(contract(pick_dy, back[h], 0, 0))
    mixed = jnp.concatenate(mixed, axis=1).astype(jnp.bfloat16)
    token_grad = jnp.concatenate(token_grad, axis=1).astype(jnp.bfloat16)
    w_gate_grad = contract(rows_x, grad_gate, 0, 0).astype(jnp.bfloat16)[None]
    w_up_grad = contract(rows_x, grad_up, 0, 0).astype(jnp.bfloat16)[None]
    w_down_grad = contract(rows_dy, hidden, 0, 0).astype(jnp.bfloat16)[None]
    return (mixed, token_grad, gate_grad, w_gate_grad, w_up_grad, w_down_grad)


def solution(mesh):
    by_token = P(("expert", "context", "dp"), None)
    by_expert = P(("expert", "context"), "dp", None)
    return jax.shard_map(
        shards,
        mesh=mesh,
        in_specs=(by_token,) * 4 + (by_expert,) * 3,
        out_specs=(by_token,) * 3 + (by_expert,) * 3,
        check_vma=False,
    )
```

time: 612 us -> 391 us (0.64)
  the two profiles are of different devices: /device:TPU:1 before, /device:TPU:33 now
where the time goes in v1:
time: 391 us; the launch traced here: 389 us
  waiting for transfers between devices  188 us (48%)
  blocking collectives  111 us (28%)
  matrix products  45.2 us (12%)
  local copies, waits for them, and re-layouts  21.2 us (5%)
  other arithmetic  13.6 us (3%)
  starting transfers between devices  8.97 us (2%)
    all_to_all x1, blocking collectives, shards(): recv = lax.all_to_all(send, PEERS, split_axis=0, concat_axis=0, tiled=True)  111 us
    ppermute x1, waiting for transfers between devices, shards(): other = lax.ppermute(mine, 'dp', swap).astype(jnp.float32)  103 us
    all_to_all x1, waiting for transfers between devices, shards(): back = lax.all_to_all(back, PEERS, split_axis=0, concat_axis=0, tiled=True)  84.4 us
    dot_general x19, matrix products, contract(): lax.dot_general(left, right, (((left_dim,), (right_dim,)), ((), ())), pre...  45.2 us
    all_to_all x1, starting transfers between devices, shards(): back = lax.all_to_all(back, PEERS, split_axis=0, concat_axis=0, tiled=True)  8.37 us
  transfers between devices with their start and end apart: 2, of which 2 were waited for; matrix products, arithmetic and copies ran while one was open for 3% of the time, Pallas kernels for 0%

profile of v1, /device:TPU:33, one launch (start us, length us, event | category | flops | bytes accessed | tf_op | source)
XLA Modules:
  0.0 388.6 jit_solution(11455289140258068028)
XLA Ops:
  0.6 0.8 slice_bitcast_fusion.14
  1.7 1.7 fusion.33
  6.4 111.0 %all_to_all.10 = bf16[256,8,1024]{2,1,0:T(8,128)(2,1)S(1)} all-to-all(bf16[256,8,1024]{2,1,0:T(8,128)(2,1)S(1)} %bitcast.72), channel_id=1, replica_groups=mesh['expert'=16,'context'=8,'dp'=2] {'dp','expert','context'}, dimensions={0} | all-to-all | bytes 8388608 | tf_op jit(solution)/shard_map/all_to_all | solution.py:49
  117.4 2.8 fusion.63
  120.2 4.0 %reshape.51 = bf16[1024,1024]{1,0:T(8,128)(2,1)} reshape(bf16[256,4,1024]{2,1,0:T(4,128)(2,1)} %get-tuple-element.13) | data formatting | bytes 4194304 | tf_op jit(solution)/shard_map/reshape | solution.py:50
  124.2 4.1 %reshape.52 = bf16[1024,1024]{1,0:T(8,128)(2,1)} reshape(bf16[256,4,1024]{2,1,0:T(4,128)(2,1)} %get-tuple-element.14) | data formatting | bytes 4194304 | tf_op jit(solution)/shard_map/reshape | solution.py:51
  128.3 3.6 fusion.65
  132.0 1.9 fusion.66
  133.9 1.9 fusion.64
  137.0 103.3 %collective-permute-done = bf16[1024,2304]{0,1:T(8,128)(2,1)S(1)} collective-permute-done((bf16[1024,2304]{0,1:T(8,128)(2,1)S(1)}, bf16[1024,2304]{0,1:T(8,128)(2,1)S(1)}, u32[]{:S(2)}, u32[]{:S(2)}) %collective-permute-start) | collective-permute-done | bytes 4718624 | tf_op jit(solution)/shard_map/ppermute | solution.py:61
  240.3 1.2 convert_element_type.79
  241.5 3.7 multiply_convert_fusion.2
  245.2 1.1 copy-done.6
  246.3 3.2 convolution_convert_fusion
  249.5 4.1 %reshape.53 = bf16[256,4,1024]{2,1,0:T(4,128)(2,1)} reshape(bf16[1024,1024]{1,0:T(8,128)(2,1)} %convolution_convert_fusion) | data formatting | bytes 4194304 | tf_op jit(solution)/shard_map/reshape | solution.py:77
  253.6 3.4 fusion.12
  257.1 3.2 add_convert_fusion
  260.3 4.2 %reshape.54 = bf16[256,4,1024]{2,1,0:T(4,128)(2,1)} reshape(bf16[1024,1024]{1,0:T(8,128)(2,1)} %add_convert_fusion) | data formatting | bytes 4194304 | tf_op jit(solution)/shard_map/reshape | solution.py:78
  264.4 4.9 %pad_maximum_fusion.2 = bf16[256,8,1024]{2,1,0:T(8,128)(2,1)} fusion(bf16[256,4,1024]{2,1,0:T(4,128)(2,1)} %reshape.54, bf16[256,4,1024]{2,1,0:T(4,128)(2,1)} %reshape.53), kind=kLoop, calls=%fused_computation.2 | loop fusion | flops 8388608 | bytes 8388608 | tf_op jit(solution)/shard_map/concatenate | solution.py:75
  269.3 8.4 %all-to-all-start.1 = ((bf16[256,8,1024]{2,1,0:T(8,128)(2,1)}), bf16[256,8,1024]{2,1,0:T(8,128)(2,1)}, u32[]{:S(2)}, u32[]{:S(2)}) async-start(bf16[256,8,1024]{2,1,0:T(8,128)(2,1)} %pad_maximum_fusion.2), calls=%async_computation.1 | async-start | bytes 8388608 | tf_op jit(solution)/shard_map/all_to_all | solution.py:82
  277.7 5.2 %fusion.21 = bf16[1,1024,768]{2,1,0:T(8,128)(2,1)} fusion(bf16[1024,1024]{1,0:T(8,128)(2,1)} %reshape.52, bf16[1024,768]{0,1:T(8,128)(2,1)} %copy-done.6), kind=kOutput, calls=%fused_computation.40 | convolution fusion | flops 1611399168 | bytes 5242880 | tf_op jit(solution)/shard_map/dot_general | solution.py:10
  282.9 3.0 fusion.19
  286.0 3.0 fusion.20
  289.0 84.4 %all-to-all-done.1 = bf16[256,8,1024]{2,1,0:T(8,128)(2,1)} async-done(((bf16[256,8,1024]{2,1,0:T(8,128)(2,1)}), bf16[256,8,1024]{2,1,0:T(8,128)(2,1)}, u32[]{:S(2)}, u32[]{:S(2)}) %all-to-all-start.1) | async-done | bytes 4194336 | tf_op jit(solution)/shard_map/all_to_all | solution.py:82
  373.4 2.1 fusion.22
  375.4 2.1 fusion.23
  377.5 0.8 pad_maximum_fusion.4
  378.4 2.1 fusion.7
  380.5 2.1 fusion.4
  382.6 2.2 fusion.5
  384.8 2.4 fusion.26
  387.2 0.8 pad_maximum_fusion.3
  (41 shorter events, 4.9 us)
Async XLA Ops:
  0.6 133.2 %copy-start = (bf16[1,1024,768]{2,1,0:T(8,128)(2,1)S(1)}, bf16[1,1024,768]{2,1,0:T(8,128)(2,1)}, u32[]{:S(2)}) copy-start(bf16[1,1024,768]{2,1,0:T(8,128)(2,1)} %param.13) | copy-start | bytes 4718596
  1.7 1.7 copy-start.7
  3.4 0.7 copy-start.10
  3.4 1.1 copy-start.8
  124.2 4.1 %copy-start.11 = (bf16[1,1024,768]{2,1,0:T(8,128)(2,1)S(1)}, bf16[1,1024,768]{2,1,0:T(8,128)(2,1)}, u32[]{:S(2)}) copy-start(bf16[1,1024,768]{2,1,0:T(8,128)(2,1)} %param.12) | copy-start | bytes 4718596
  128.3 3.6 copy-start.2
  128.3 3.6 copy-start.12
  132.0 1.9 copy-start.4
  136.4 103.9 %collective-permute-start = (bf16[1024,2304]{0,1:T(8,128)(2,1)S(1)}, bf16[1024,2304]{0,1:T(8,128)(2,1)S(1)}, u32[]{:S(2)}, u32[]{:S(2)}) collective-permute-start(bf16[1024,2304]{0,1:T(8,128)(2,1)S(1)} %pad_maximum_fusion), channel_id=1, source_target_pairs={{0,1},{1,0},{2,3},{3,2},{4,5},{5,4},{6,7},{7,6},{8,9},{9,8},{10,11... | collective-permute-start | bytes 14155784 | tf_op jit(solution)/shard_map/ppermute | solution.py:61
  245.2 1.1 copy-start.6
  253.6 3.4 copy-start.5
  253.6 3.4 copy-start.13
  269.3 104.0 %all-to-all-start.1 = ((bf16[256,8,1024]{2,1,0:T(8,128)(2,1)}), bf16[256,8,1024]{2,1,0:T(8,128)(2,1)}, u32[]{:S(2)}, u32[]{:S(2)}) async-start(bf16[256,8,1024]{2,1,0:T(8,128)(2,1)} %pad_maximum_fusion.2), calls=%async_computation.1 | async-start | bytes 8388608 | tf_op jit(solution)/shard_map/all_to_all | solution.py:82
  277.7 5.2 %copy-start.3 = (bf16[1024,1024]{1,0:T(8,128)(2,1)S(1)}, bf16[1024,1024]{1,0:T(8,128)(2,1)}, u32[]{:S(2)}) copy-start(bf16[1024,1024]{1,0:T(8,128)(2,1)} %reshape.51) | copy-start | bytes 6291460
  382.5 2.3 copy-start.9
  382.6 6.1 %copy-start.1 = (bf16[1,1024,768]{2,1,0:T(8,128)(2,1)S(1)}, bf16[1,1024,768]{2,1,0:T(8,128)(2,1)}, u32[]{:S(2)}) copy-start(bf16[1,1024,768]{2,1,0:T(8,128)(2,1)} %param.13) | copy-start | bytes 4718596

commit v2 on v1

v2 whole, which is shorter than its diff:
```python
import functools

import jax
import jax.numpy as jnp
from jax import lax
from jax.experimental import pallas as pl
from jax.experimental.pallas import tpu as pltpu
from jax.sharding import PartitionSpec as P

MESH = pl.DeviceIdType.MESH
X, Y, Z = 4, 4, 8
PLANE = X * Y * 2
ROWS = 8 * PLANE


def contract(left, right, left_dim, right_dim):
    return lax.dot_general(
        left, right, (((left_dim,), (right_dim,)), ((), ())), preferred_element_type=jnp.float32
    )


def plane_order(z, g):
    pair = (z // 2 + (g // 2 % 2) * 2 + g // 4) % (Z // 2)
    return pair * 2 + g % 2


def experts_kernel(
    send_ref, gate_ref, up_ref, down_ref, back_ref, gate_out, up_out, down_out,
    recv, relay, own_a, own_b, mine, other, ret, relay_back, terms,
    recv_sem, send_sem, relay_sem, forward_sem, mine_sem, other_sem,
    ret_sem, relay_back_sem, forward_back_sem, back_sem,
):
    expert, context, z_lo = (lax.axis_index(a) for a in ("expert", "context", "dp"))
    x, y, core = expert // Y, expert % Y, context % 2
    z = context // 2 * 2 + z_lo
    ff = gate_ref.shape[1]
    half = ff // 2

    def device(x, y, z, core):
        return (x * Y + y, z // 2 * 2 + core, z % 2)

    def place(x, y, z, core):
        return z % 2 * 128 + (x * Y + y) * 8 + z // 2 * 2 + core

    def peer(j):
        return (x + j % X) % X, (y + j // X % Y) % Y, (core + j // (X * Y)) % 2

    me = place(x, y, z, core)
    my_slot = z * PLANE + expert * 2 + core

    barrier = pltpu.get_barrier_semaphore()

    def greet(i, _):
        g, j = i // PLANE, i % PLANE
        px, py, pc = peer(j)
        to = device(px, py, (z + g) % Z, pc)
        pl.semaphore_signal(barrier, inc=1, device_id=to, device_id_type=MESH)
        return 0

    lax.fori_loop(1, Z * PLANE, greet, 0)
    pl.semaphore_wait(barrier, Z * PLANE - 1)

    def push(src, dst, sent, arrived, to):
        pltpu.make_async_remote_copy(
            src_ref=src, dst_ref=dst, send_sem=sent, recv_sem=arrived, device_id=to, device_id_type=MESH
        ).start()

    opposite = (z + Z // 2) % Z
    before, beyond = (z + Z - 1) % Z, (z + 1) % Z

    def by_relay(block, relay_to, sent, arrived):
        def one(j, _):
            px, py = (x + j % X) % X, (y + j // X) % Y
            push(block(px, py, opposite, 1), relay_to.at[px * Y + py], sent, arrived,
                 device(x, y, before, core))
            return 0

        lax.fori_loop(0, X * Y, one, 0)

    def forward(relay_from, dst, sent, arrived):
        def one(j, _):
            px, py = (x + j % X) % X, (y + j // X) % Y
            push(relay_from.at[px * Y + py], dst, sent, arrived,
                 device(px, py, (beyond + Z // 2) % Z, 1))
            return 0

        lax.fori_loop(0, X * Y, one, 0)

    def to_plane(plane, block, dst, sent, arrived):
        def one(j, _):
            px, py, pc = peer(j)

            @pl.when((plane != z) | (j > 0))
            def _():
                @pl.when((plane != opposite) | (pc == 0))
                def _():
                    push(block(px, py, plane, pc), dst, sent, arrived, device(px, py, plane, pc))

            return 0

        lax.fori_loop(0, PLANE, one, 0)

    def wait(ref, sem):
        pltpu.make_async_copy(ref, ref, sem).wait()

    def out_block(px, py, pz, pc):
        return send_ref.at[place(px, py, pz, pc)]

    by_relay(out_block, relay, send_sem, relay_sem)
    pltpu.make_async_copy(send_ref.at[me], recv.at[my_slot], recv_sem.at[z]).start()

    def dispatch(g, _):
        to_plane(plane_order(z, g), out_block, recv.at[my_slot], send_sem, recv_sem.at[z])
        return 0

    lax.fori_loop(0, 4, dispatch, 0)
    wait(relay, relay_sem)
    forward(relay, recv.at[beyond * PLANE + expert * 2 + core], forward_sem, recv_sem.at[beyond])
    lax.fori_loop(4, Z, dispatch, 0)

    token_row = lax.broadcasted_iota(jnp.int32, (ROWS, half), 0) % 8 < 4

    def rows_of(value):
        return value.astype(jnp.float32).reshape(-1, value.shape[-1])

    def partial_sums(g, _):
        plane = plane_order(z, g)
        here = pl.ds(pl.multiple_of(plane * PLANE, PLANE), PLANE)
        wait(recv.at[here], recv_sem.at[plane])
        rows = rows_of(recv[here]).astype(jnp.bfloat16)
        for h in range(2):
            cols = slice(h * half, (h + 1) * half)
            part = jnp.where(
                token_row,
                contract(rows, gate_ref[:, cols], 1, 0),
                contract(rows, down_ref[:, cols], 1, 0),
            )
            own_a[plane, :, cols] = part
            mine[plane, :, cols] = part.astype(jnp.bfloat16)
        part = jnp.where(
            token_row,
            contract(rows, up_ref[:, :half], 1, 0),
            pltpu.roll(contract(rows, up_ref[:, half:], 1, 0), 4, 0),
        )
        own_b[plane] = part
        mine[plane, :, ff:] = part.astype(jnp.bfloat16)
        push(mine.at[plane], other.at[plane], mine_sem, other_sem.at[plane],
             (expert, context, 1 - z_lo))
        return 0

    lax.fori_loop(0, Z, partial_sums, 0)

    def back_block(px, py, pz, pc):
        return ret.at[pz * PLANE + (px * Y + py) * 2 + pc]

    def finish(g, _):
        plane = plane_order(z, g)
        wait(other.at[plane], other_sem.at[plane])
        up_two = own_b[plane] + other[plane, :, ff:].astype(jnp.float32)
        total = jnp.zeros((ROWS, gate_ref.shape[0]), jnp.float32)
        at = pl.ds(pl.multiple_of(plane * ROWS, ROWS), ROWS)
        for h in range(2):
            cols = slice(h * half, (h + 1) * half)
            both = own_a[plane, :, cols] + other[plane, :, cols].astype(jnp.float32)
            gate_pre = jnp.where(token_row, both, pltpu.roll(both, 4, 0))
            if h == 0:
                up_pre = jnp.where(token_row, up_two, pltpu.roll(up_two, 4, 0))
            else:
                up_pre = jnp.where(token_row, pltpu.roll(up_two, ROWS - 4, 0), up_two)
            sig_gate = jax.nn.sigmoid(gate_pre)
            active = gate_pre * sig_gate
            slope = sig_gate * (1.0 + gate_pre * (1.0 - sig_gate))
            hidden = jnp.where(token_row, active * up_pre, 0.0)
            grad_gate = jnp.where(token_row, 0.0, both * up_pre * slope)
            grad_up = jnp.where(token_row, 0.0, both * active)
            total += contract(hidden.astype(jnp.bfloat16), down_ref[:, cols], 1, 1)
            total += contract(grad_gate.astype(jnp.bfloat16), gate_ref[:, cols], 1, 1)
            total += contract(grad_up.astype(jnp.bfloat16), up_ref[:, cols], 1, 1)
            terms[at, h * half : (h + 1) * half] = pltpu.roll(grad_gate, ROWS - 4, 0).astype(
                jnp.bfloat16
            )
            terms[at, ff + h * half : ff + (h + 1) * half] = pltpu.roll(
                grad_up, ROWS - 4, 0
            ).astype(jnp.bfloat16)
            terms[at, 2 * ff + h * half : 2 * ff + (h + 1) * half] = pltpu.roll(
                hidden, 4, 0
            ).astype(jnp.bfloat16)
        here = pl.ds(pl.multiple_of(plane * PLANE, PLANE), PLANE)
        ret[here] = total.reshape(PLANE, 8, total.shape[-1]).astype(jnp.bfloat16)

        @pl.when(plane == z)
        def _():
            pltpu.make_async_copy(ret.at[my_slot], back_ref.at[me], back_sem).start()

        @pl.when(plane == opposite)
        def _():
            by_relay(back_block, relay_back, ret_sem, relay_back_sem)

        to_plane(plane, back_block, back_ref.at[me], ret_sem, back_sem)
        return 0

    lax.fori_loop(0, 6, finish, 0)
    wait(relay_back, relay_back_sem)
    forward(relay_back, back_ref.at[place(x, y, beyond, core)], forward_back_sem, back_sem)
    lax.fori_loop(6, Z, finish, 0)

    step = 256

    def weight_grads(i, _):
        cols = pl.ds(pl.multiple_of(i * step, step), step)
        rows = rows_of(recv[:, :, cols]).T.astype(jnp.bfloat16)
        for n, out in enumerate((gate_out, up_out, down_out)):
            out[cols, :] = contract(rows, terms[:, n * ff : (n + 1) * ff], 1, 0).astype(jnp.bfloat16)
        return 0

    lax.fori_loop(0, gate_ref.shape[0] // step, weight_grads, 0)

    wait(recv.at[pl.ds(0, Z * PLANE - 1)], send_sem)
    wait(relay, forward_sem)
    wait(mine, mine_sem)
    wait(ret.at[pl.ds(0, Z * PLANE - 1)], ret_sem)
    wait(relay_back, forward_back_sem)
    wait(back_ref, back_sem)


def through_experts(send, gate_w, up_w, down_w):
    width, ff = gate_w.shape
    vmem = pl.BlockSpec(memory_space=pltpu.VMEM)
    hbm = pl.BlockSpec(memory_space=pl.ANY)
    bf16, f32, dma = jnp.bfloat16, jnp.float32, pltpu.SemaphoreType.DMA
    weight = jax.ShapeDtypeStruct((width, ff), bf16)
    return pl.pallas_call(
        experts_kernel,
        out_shape=(jax.ShapeDtypeStruct(send.shape, bf16), weight, weight, weight),
        in_specs=[hbm, vmem, vmem, vmem],
        out_specs=(hbm, vmem, vmem, vmem),
        scratch_shapes=[
            pltpu.VMEM(send.shape, bf16),
            pltpu.VMEM((X * Y,) + send.shape[1:], bf16),
            pltpu.VMEM((Z, ROWS, ff), f32),
            pltpu.VMEM((Z, ROWS, ff // 2), f32),
            pltpu.VMEM((Z, ROWS, ff + ff // 2), bf16),
            pltpu.VMEM((Z, ROWS, ff + ff // 2), bf16),
            pltpu.VMEM(send.shape, bf16),
            pltpu.VMEM((X * Y,) + send.shape[1:], bf16),
            pltpu.VMEM((Z * ROWS, 3 * ff), bf16),
            dma((Z,)), dma, dma, dma, dma, dma((Z,)), dma, dma, dma, dma,
        ],
        compiler_params=pltpu.CompilerParams(
            collective_id=0, has_side_effects=True, vmem_limit_bytes=63_000_000
        ),
    )(send, gate_w, up_w, down_w)


def shards(tokens, routes, gates, out_grad, w_gate, w_up, w_down):
    experts = lax.axis_size(("expert", "context"))
    halves = lax.axis_size("dp")
    devices = experts * halves
    local_tokens, top_count = routes.shape
    width = tokens.shape[1] // halves
    capacity = max(2, 2 * local_tokens * top_count // experts)
    block = 2 * capacity

    slots = jnp.concatenate([routes[:, k] for k in range(top_count)])
    count = slots.shape[0]
    order = lax.broadcasted_iota(jnp.int32, (count, count), 0)
    before = lax.broadcasted_iota(jnp.int32, (count, count), 1) < order
    place = jnp.sum(((slots[:, None] == slots[None, :]) & before).astype(jnp.int32), axis=1)
    place = (slots * block + place).reshape(top_count, local_tokens)
    rows = lax.broadcasted_iota(jnp.int32, (experts * block, local_tokens), 0)
    hits_x = [rows == place[k][None, :] for k in range(top_count)]
    hits_dy = [rows == place[k][None, :] + capacity for k in range(top_count)]
    pick_x = sum(h.astype(jnp.bfloat16) for h in hits_x)
    pick_dy = sum(h.astype(jnp.bfloat16) for h in hits_dy)
    gate_of = sum(
        jnp.sum(jnp.where(h, gates[:, k][None, :], 0.0), axis=1) for k, h in enumerate(hits_dy)
    )

    def half(array, h):
        return array[:, h * width : (h + 1) * width]

    sends = []
    for h in range(halves):
        picked = contract(pick_x, half(tokens, h), 1, 0)
        graded = gate_of[:, None] * contract(pick_dy, half(out_grad, h), 1, 0)
        sends.append((picked + graded).astype(jnp.bfloat16))
    send = jnp.stack(sends).reshape(devices, block, width)
    back, w_gate_grad, w_up_grad, w_down_grad = through_experts(
        send, w_gate[0], w_up[0], w_down[0]
    )
    back = back.reshape(halves, experts * block, width)
    mixed, token_grad, gate_grad = [], [], 0.0
    for h in range(halves):
        outs = [contract(x.astype(jnp.bfloat16), back[h], 0, 0) for x in hits_x]
        cot = half(out_grad, h).astype(jnp.float32)
        mixed.append(sum(gates[:, k][:, None] * out for k, out in enumerate(outs)))
        gate_grad += jnp.stack([jnp.sum(out * cot, axis=1) for out in outs], axis=1)
        token_grad.append(contract(pick_dy, back[h], 0, 0))
    mixed = jnp.concatenate(mixed, axis=1).astype(jnp.bfloat16)
    token_grad = jnp.concatenate(token_grad, axis=1).astype(jnp.bfloat16)
    return (mixed, token_grad, gate_grad, w_gate_grad[None], w_up_grad[None], w_down_grad[None])


def solution(mesh):
    by_token = P(("expert", "context", "dp"), None)
    by_expert = P(("expert", "context"), "dp", None)
    return jax.shard_map(
        shards,
        mesh=mesh,
        in_specs=(by_token,) * 4 + (by_expert,) * 3,
        out_specs=(by_token,) * 3 + (by_expert,) * 3,
        check_vma=False,
    )
```

time: 391 us -> 354 us (0.905)
  Pallas kernels: 0 us -> 333 us
  waiting for transfers between devices: 188 us -> 0 us
  blocking collectives: 111 us -> 0 us
  matrix products: 45.2 us -> 10.3 us
  local copies, waits for them, and re-layouts: 21.2 us -> 5.28 us
  starting transfers between devices: 8.97 us -> 0 us
  other arithmetic: 13.6 us -> 5.07 us
    pallas_call x0 -> x1, Pallas kernels: none -> 333 us  [through_experts(): pl.pallas_call(experts_kernel, out_shape=(jax.ShapeDtypeStruct(send.shape...]
    all_to_all x1 -> x0, blocking collectives: 111 us -> none  [shards(): recv = lax.all_to_all(send, PEERS, split_axis=0, concat_axis=0, tiled=True)]
    ppermute x1 -> x0, waiting for transfers between devices: 103 us -> none  [shards(): other = lax.ppermute(mine, 'dp', swap).astype(jnp.float32)]
    all_to_all x1 -> x0, waiting for transfers between devices: 84.4 us -> none  [shards(): back = lax.all_to_all(back, PEERS, split_axis=0, concat_axis=0, tiled=True)]
    dot_general x19 -> x10, matrix products: 45.2 us -> 10.3 us  [contract(): lax.dot_general(left, right, (((left_dim,), (right_dim,)), ((), ())), pre...]
    reshape x4 -> x0, local copies, waits for them, and re-layouts: 16.4 us -> none  [the longest x1 4.17 us: shards(): expert_dx.reshape(devices, capacity, width)]
    all_to_all x1 -> x0, starting transfers between devices: 8.37 us -> none  [shards(): back = lax.all_to_all(back, PEERS, split_axis=0, concat_axis=0, tiled=True)]
    concatenate x2 -> x0, other arithmetic: 5.51 us -> none  [the longest x1 4.91 us: shards(): jnp.concatenate([expert_out.reshape(devices, capacity, width), expert_dx....]
  transfers between devices with their start and end apart: 2 -> 0, of which waited for: 2 -> 0; matrix products, arithmetic and copies ran while one was open for 3% -> 0% of each run, Pallas kernels for 0% -> 0%
where the time goes in v2:
time: 354 us
  Pallas kernels  333 us (94%)
  matrix products  10.3 us (3%)
  local copies, waits for them, and re-layouts  5.28 us (1%)
  other arithmetic  5.07 us (1%)
    pallas_call x1, Pallas kernels, through_experts(): pl.pallas_call(experts_kernel, out_shape=(jax.ShapeDtypeStruct(send.shape...  333 us
    dot_general x10, matrix products, contract(): lax.dot_general(left, right, (((left_dim,), (right_dim,)), ((), ())), pre...  10.3 us

profile of v2, /device:TPU:33, one launch (start us, length us, event | category | flops | bytes accessed | tf_op | source)
XLA Modules:
  0.0 354.1 jit_solution(5236593885540406338)
XLA Ops:
  0.6 0.0 copy-start.4
  0.6 0.8 slice_bitcast_fusion.2
  1.4 0.2 convert_reduce_fusion
  1.6 0.8 slice_bitcast_fusion
  2.4 0.3 select_reduce_fusion
  2.7 1.6 fusion.35
  4.4 0.0 copy-done.4
  4.4 0.0 copy-start.3
  4.4 0.7 fusion.13
  5.1 0.3 copy-done.3
  5.4 0.7 fusion.37
  6.1 0.7 fusion.12
  6.9 2.3 pad_maximum_fusion
  9.2 332.7 %shard_map.118 = (bf16[256,8,1024]{2,1,0:T(8,128)(2,1)}, bf16[1024,768]{1,0:T(8,128)(2,1)}, bf16[1024,768]{1,0:T(8,128)(2,1)}, bf16[1024,768]{1,0:T(8,128)(2,1)}) custom-call(bf16[256,8,1024]{2,1,0:T(8,128)(2,1)} %bitcast.43, bf16[1024,768]{1,0:T(8,128)(2,1)} %bitcast.47, bf16[1024,768]{1,0:T(8,128)(2,1)} %bitcast.48, bf16[1024,768]{1,0:T(8,128)(2,1)} %bitcast.49), custom_call_target="tpu_custom_call" | custom-call | tf_op jit(solution)/shard_map/pallas_call | solution.py:232
  341.8 0.0 copy-start.5
  341.8 2.2 fusion.20
  344.1 2.1 fusion.23
  346.1 0.8 pad_maximum_fusion.2
  347.0 0.0 copy-done.5
  347.0 0.5 fusion.8
  347.5 0.5 fusion.2
  348.0 0.0 copy-start.2
  348.0 0.5 fusion.10
  348.5 0.0 copy-start.1
  348.5 0.8 fusion.28
  349.3 0.6 maximum_add_fusion
  349.9 0.8 pad_maximum_fusion.1
  350.7 0.0 copy-done.2
  350.7 1.1 copy.16
  351.9 0.0 copy-done.1
  351.9 1.1 copy.17
  353.0 1.1 copy.18
  (6 shorter events, 0.0 us)
Async XLA Ops:
  0.6 3.8 %copy-start.4 = (bf16[128,2048]{1,0:T(8,128)(2,1)S(1)}, bf16[128,2048]{1,0:T(8,128)(2,1)}, u32[]{:S(2)}) copy-start(bf16[128,2048]{1,0:T(8,128)(2,1)} %param.10) | copy-start | bytes 1572868
  4.4 1.0 copy-start.3
  341.8 5.2 %copy-start.5 = (bf16[256,8,1024]{2,1,0:T(8,128)(2,1)S(1)}, bf16[256,8,1024]{2,1,0:T(8,128)(2,1)}, u32[]{:S(2)}) copy-start(bf16[256,8,1024]{2,1,0:T(8,128)(2,1)} %get-tuple-element.10) | copy-start | bytes 12582916
  348.0 2.7 copy-start.2
  348.5 3.4 copy-start.1
  349.3 3.7 %copy-start = (bf16[1024,768]{1,0:T(8,128)(2,1)S(1)}, bf16[1024,768]{1,0:T(8,128)(2,1)}, u32[]{:S(2)}) copy-start(bf16[1024,768]{1,0:T(8,128)(2,1)} %get-tuple-element.13) | copy-start | bytes 4718596

commit v3 on v2

v3 whole, which is shorter than its diff:
```python
import jax
import jax.numpy as jnp
from jax import lax
from jax.experimental import pallas as pl
from jax.experimental.pallas import tpu as pltpu
from jax.sharding import PartitionSpec as P

MESH = pl.DeviceIdType.MESH
X, Y, Z = 4, 4, 8
PLANE = X * Y * 2
ROWS = 8 * PLANE


def contract(left, right, left_dim, right_dim):
    return lax.dot_general(
        left, right, (((left_dim,), (right_dim,)), ((), ())), preferred_element_type=jnp.float32
    )


def plane_order(z, g):
    pair = (z // 2 + (g // 2 % 2) * 2 + g // 4) % (Z // 2)
    return pair * 2 + g % 2


def return_order(z, g):
    pair = (z // 2 + (g // 2 % 2) * 2 + g // 4 * 3) % (Z // 2)
    return pair * 2 + g % 2


def places(one, other_way, axis):
    token = lax.broadcasted_iota(jnp.int32, (one[0].size, one[0].size), axis)
    earlier = token < lax.broadcasted_iota(jnp.int32, token.shape, 1 - axis)
    found = []
    for k, expert in enumerate(one):
        place = 0
        for n in range(k + 1):
            same = other_way[n] == expert
            same = same & earlier if n == k else same
            place += jnp.sum(same.astype(jnp.int32), axis=axis, keepdims=True)
        block = (expert // 2 % 4) * (2 * X * Y) * 2 + expert // 8 * 2 + expert % 2
        found.append(block * 8 + place)
    return found


def experts_kernel(
    tokens_ref, grad_ref, routes_ref, routes_t_ref, gates_ref, gates_t_ref, gate_ref, up_ref, down_ref,
    mixed_out, token_out, grad_out, gate_out, up_out, down_out,
    recv, own_a, own_b, mine, other, send, back, terms, sum_0, sum_1, sum_dx,
    recv_sem, self_sem, send_sem, mine_sem, other_sem, ret_sem, back_sem,
):
    expert, context, z_lo = (lax.axis_index(a) for a in ("expert", "context", "dp"))
    x, y, core = expert // Y, expert % Y, context % 2
    z = context // 2 * 2 + z_lo
    width, ff = gate_ref.shape
    half = ff // 2

    def device(x, y, z, core):
        return (x * Y + y, z // 2 * 2 + core, z % 2)

    def peer(j):
        return (x + j % X) % X, (y + j // X % Y) % Y, (core + j // (X * Y)) % 2

    my_slot = z * PLANE + expert * 2 + core

    barrier = pltpu.get_barrier_semaphore()

    def greet(i, _):
        g, j = i // PLANE, i % PLANE
        px, py, pc = peer(j)
        to = device(px, py, (z + g) % Z, pc)
        pl.semaphore_signal(barrier, inc=1, device_id=to, device_id_type=MESH)
        return 0

    lax.fori_loop(1, Z * PLANE, greet, 0)

    routes_col = [routes_ref[:, k : k + 1] for k in range(2)]
    routes_row = [routes_t_ref[k : k + 1, :] for k in range(2)]
    place_row = places(routes_row, routes_col, 0)
    place_col = places(routes_col, routes_row, 1)
    gates_row = [gates_t_ref[k : k + 1, :] for k in range(2)]
    tokens_here = tokens_ref.shape[0]
    sum_0[...] = jnp.zeros_like(sum_0)
    sum_1[...] = jnp.zeros_like(sum_1)
    sum_dx[...] = jnp.zeros_like(sum_dx)

    pl.semaphore_wait(barrier, Z * PLANE - 1)

    def push(src, dst, sent, arrived, to):
        pltpu.make_async_remote_copy(
            src_ref=src, dst_ref=dst, send_sem=sent, recv_sem=arrived, device_id=to, device_id_type=MESH
        ).start()

    def to_plane(plane, dst, sent, arrived):
        def one(j, _):
            px, py, pc = peer(j)

            @pl.when((plane != z) | (j > 0))
            def _():
                src = send.at[plane * PLANE + (px * Y + py) * 2 + pc]
                push(src, dst, sent, arrived, device(px, py, plane, pc))

            return 0

        lax.fori_loop(0, PLANE, one, 0)

    def wait(ref, sem):
        pltpu.make_async_copy(ref, ref, sem).wait()

    def blocks_of(plane):
        return pl.ds(pl.multiple_of(plane * PLANE, PLANE), PLANE)

    def columns_of(plane):
        return pl.ds(pl.multiple_of(plane % 2 * width, width), width)

    def rows_of(value):
        return value.astype(jnp.float32).reshape(-1, value.shape[-1])

    def dispatch(g, _):
        plane = plane_order(z, g)
        first = plane // 2 * (2 * ROWS)
        row = lax.broadcasted_iota(jnp.int32, (ROWS, tokens_here), 0) + first
        hits = [row == place for place in place_row]
        hits_dy = [row == place + 4 for place in place_row]
        pick = sum(h.astype(jnp.float32) for h in hits).astype(jnp.bfloat16)
        pick_dy = sum(h.astype(jnp.float32) for h in hits_dy).astype(jnp.bfloat16)
        gate_of = sum(
            jnp.sum(jnp.where(h, gate, 0.0), axis=1, keepdims=True)
            for h, gate in zip(hits_dy, gates_row, strict=True)
        )
        cols = columns_of(plane)
        block = contract(pick, tokens_ref[:, cols], 1, 0)
        block += gate_of * contract(pick_dy, grad_ref[:, cols], 1, 0)
        send[blocks_of(plane)] = block.reshape(PLANE, 8, width).astype(jnp.bfloat16)

        @pl.when(plane == z)
        def _():
            pltpu.make_async_copy(send.at[my_slot], recv.at[my_slot], self_sem).start()

        to_plane(plane, recv.at[my_slot], send_sem, recv_sem.at[z])
        return 0

    lax.fori_loop(0, Z, dispatch, 0)

    token_row = lax.broadcasted_iota(jnp.int32, (ROWS, half), 0) % 8 < 4

    def wait_plane(buffer, plane, sem):
        @pl.when(plane == z)
        def _():
            wait(buffer.at[my_slot], self_sem)
            wait(buffer.at[pl.ds(0, PLANE - 1)], sem.at[plane])

        @pl.when(plane != z)
        def _():
            wait(buffer.at[pl.ds(0, PLANE)], sem.at[plane])

    def partial_sums(g, _):
        plane = plane_order(z, g)
        wait_plane(recv, plane, recv_sem)
        rows = rows_of(recv[blocks_of(plane)]).astype(jnp.bfloat16)
        for h in range(2):
            cols = slice(h * half, (h + 1) * half)
            part = jnp.where(
                token_row,
                contract(rows, gate_ref[:, cols], 1, 0),
                contract(rows, down_ref[:, cols], 1, 0),
            )
            own_a[plane, :, cols] = part
            mine[plane, :, cols] = part.astype(jnp.bfloat16)
        part = jnp.where(
            token_row,
            contract(rows, up_ref[:, :half], 1, 0),
            pltpu.roll(contract(rows, up_ref[:, half:], 1, 0), 4, 0),
        )
        own_b[plane] = part
        mine[plane, :, ff:] = part.astype(jnp.bfloat16)
        push(mine.at[plane], other.at[plane], mine_sem, other_sem.at[plane],
             (expert, context, 1 - z_lo))
        return 0

    lax.fori_loop(0, Z, partial_sums, 0)
    wait(send.at[pl.ds(0, Z * PLANE - 1)], send_sem)

    def finish(g, _):
        plane = plane_order(z, g)
        wait(other.at[plane], other_sem.at[plane])
        up_two = own_b[plane] + other[plane, :, ff:].astype(jnp.float32)
        total = jnp.zeros((ROWS, width), jnp.float32)
        at = pl.ds(pl.multiple_of(plane * ROWS, ROWS), ROWS)
        for h in range(2):
            cols = slice(h * half, (h + 1) * half)
            both = own_a[plane, :, cols] + other[plane, :, cols].astype(jnp.float32)
            gate_pre = jnp.where(token_row, both, pltpu.roll(both, 4, 0))
            if h == 0:
                up_pre = jnp.where(token_row, up_two, pltpu.roll(up_two, 4, 0))
            else:
                up_pre = jnp.where(token_row, pltpu.roll(up_two, ROWS - 4, 0), up_two)
            sig_gate = jax.nn.sigmoid(gate_pre)
            active = gate_pre * sig_gate
            slope = sig_gate * (1.0 + gate_pre * (1.0 - sig_gate))
            hidden = jnp.where(token_row, active * up_pre, 0.0)
            grad_gate = jnp.where(token_row, 0.0, both * up_pre * slope)
            grad_up = jnp.where(token_row, 0.0, both * active)
            total += contract(hidden.astype(jnp.bfloat16), down_ref[:, cols], 1, 1)
            total += contract(grad_gate.astype(jnp.bfloat16), gate_ref[:, cols], 1, 1)
            total += contract(grad_up.astype(jnp.bfloat16), up_ref[:, cols], 1, 1)
            for n, (term, shift) in enumerate(
                ((grad_gate, ROWS - 4), (grad_up, ROWS - 4), (hidden, 4))
            ):
                terms[at, n * ff + h * half : n * ff + (h + 1) * half] = pltpu.roll(
                    term, shift, 0
                ).astype(jnp.bfloat16)
        send[blocks_of(plane)] = total.reshape(PLANE, 8, width).astype(jnp.bfloat16)

        @pl.when(plane == z)
        def _():
            pltpu.make_async_copy(send.at[my_slot], back.at[my_slot], self_sem).start()

        to_plane(plane, back.at[my_slot], ret_sem, back_sem.at[z])
        return 0

    lax.fori_loop(0, Z, finish, 0)

    step = 256

    def weight_grads(i, _):
        cols = pl.ds(pl.multiple_of(i * step, step), step)
        rows = rows_of(recv[:, :, cols]).T.astype(jnp.bfloat16)
        for n, out in enumerate((gate_out, up_out, down_out)):
            out[cols, :] = contract(rows, terms[:, n * ff : (n + 1) * ff], 1, 0).astype(jnp.bfloat16)
        return 0

    lax.fori_loop(0, width // step, weight_grads, 0)

    def combine(g, _):
        plane = return_order(z, g)
        wait_plane(back, plane, back_sem)
        rows = rows_of(back[blocks_of(plane)]).astype(jnp.bfloat16)
        first = plane // 2 * (2 * ROWS)
        col = lax.broadcasted_iota(jnp.int32, (tokens_here, ROWS), 1) + first
        hits = [(col == place).astype(jnp.float32) for place in place_col]
        hits.append(sum((col == place + 4).astype(jnp.float32) for place in place_col))
        cols = columns_of(plane)
        for hit, into in zip(hits, (sum_0, sum_1, sum_dx), strict=True):
            into[:, cols] += contract(hit.astype(jnp.bfloat16), rows, 1, 0)
        return 0

    lax.fori_loop(0, Z, combine, 0)
    out_grad = grad_ref[...].astype(jnp.float32)
    mixed_out[...] = (
        gates_ref[:, 0:1] * sum_0[...] + gates_ref[:, 1:2] * sum_1[...]
    ).astype(jnp.bfloat16)
    token_out[...] = sum_dx[...].astype(jnp.bfloat16)
    grad_out[:, 0:1] = jnp.sum(sum_0[...] * out_grad, axis=1, keepdims=True)
    grad_out[:, 1:2] = jnp.sum(sum_1[...] * out_grad, axis=1, keepdims=True)

    wait(mine, mine_sem)
    wait(send.at[pl.ds(0, Z * PLANE - 1)], ret_sem)


def shards(tokens, routes, gates, out_grad, w_gate, w_up, w_down):
    _, width, ff = w_gate.shape
    bf16, f32, dma = jnp.bfloat16, jnp.float32, pltpu.SemaphoreType.DMA
    blocks = (Z * PLANE, 8, width)
    weight = jax.ShapeDtypeStruct((width, ff), bf16)
    mixed, token_grad, gate_grad, w_gate_grad, w_up_grad, w_down_grad = pl.pallas_call(
        experts_kernel,
        out_shape=(
            jax.ShapeDtypeStruct(tokens.shape, bf16),
            jax.ShapeDtypeStruct(tokens.shape, bf16),
            jax.ShapeDtypeStruct(gates.shape, f32),
            weight, weight, weight,
        ),
        in_specs=[pl.BlockSpec(memory_space=pltpu.VMEM)] * 9,
        out_specs=(pl.BlockSpec(memory_space=pltpu.VMEM),) * 6,
        scratch_shapes=[
            pltpu.VMEM(blocks, bf16),
            pltpu.VMEM((Z, ROWS, ff), f32),
            pltpu.VMEM((Z, ROWS, ff // 2), f32),
            pltpu.VMEM((Z, ROWS, ff + ff // 2), bf16),
            pltpu.VMEM((Z, ROWS, ff + ff // 2), bf16),
            pltpu.VMEM(blocks, bf16),
            pltpu.VMEM(blocks, bf16),
            pltpu.VMEM((Z * ROWS, 3 * ff), bf16),
            pltpu.VMEM(tokens.shape, f32),
            pltpu.VMEM(tokens.shape, f32),
            pltpu.VMEM(tokens.shape, f32),
            dma((Z,)), dma, dma, dma, dma((Z,)), dma, dma((Z,)),
        ],
        compiler_params=pltpu.CompilerParams(
            collective_id=0, has_side_effects=True, vmem_limit_bytes=67_043_328
        ),
    )(tokens, out_grad, routes, routes.T, gates, gates.T, w_gate[0], w_up[0], w_down[0])
    return (mixed, token_grad, gate_grad, w_gate_grad[None], w_up_grad[None], w_down_grad[None])


def solution(mesh):
    by_token = P(("expert", "context", "dp"), None)
    by_expert = P(("expert", "context"), "dp", None)
    return jax.shard_map(
        shards,
        mesh=mesh,
        in_specs=(by_token,) * 4 + (by_expert,) * 3,
        out_specs=(by_token,) * 3 + (by_expert,) * 3,
        check_vma=False,
    )
```

time: 354 us -> 330 us (0.932)
  Pallas kernels: 333 us -> 316 us
  matrix products: 10.3 us -> 0 us
  local copies, waits for them, and re-layouts: 5.28 us -> 13.3 us
  other arithmetic: 5.07 us -> 0 us
    pallas_call x1, Pallas kernels: 333 us -> 316 us  [shards(): pl.pallas_call(experts_kernel, out_shape=(jax.ShapeDtypeStruct(tokens.sha...]
    dot_general x10 -> x0, matrix products: 10.3 us -> none  [contract(): lax.dot_general(left, right, (((left_dim,), (right_dim,)), ((), ())), pre...]
    unnamed x15 -> x14, local copies, waits for them, and re-layouts: 3.77 us -> 13.3 us
where the time goes in v3:
time: 330 us
  Pallas kernels  316 us (96%)
  local copies, waits for them, and re-layouts  13.3 us (4%)
    pallas_call x1, Pallas kernels, shards(): pl.pallas_call(experts_kernel, out_shape=(jax.ShapeDtypeStruct(tokens.sha...  316 us
    unnamed x14, local copies, waits for them, and re-layouts  13.3 us

profile of v3, /device:TPU:33, one launch (start us, length us, event | category | flops | bytes accessed | tf_op | source)
XLA Modules:
  0.0 329.8 jit_solution(15106968307726690862)
XLA Ops:
  0.6 1.4 copy.13.routes_ref
  2.0 1.4 copy.14.gates_ref
  3.5 315.9 %shard_map.118 = (bf16[128,2048]{1,0:T(8,128)(2,1)}, bf16[128,2048]{1,0:T(8,128)(2,1)}, f32[128,2]{1,0:T(8,128)}, bf16[1024,768]{1,0:T(8,128)(2,1)}, bf16[1024,7...) custom-call(bf16[128,2048]{1,0:T(8,128)(2,1)} %tokens_ref.1, bf16[128,2048]{1,0:T(8,128)(2,1)} %grad_ref.1, ...), custom_call_target="tpu_custom_call" | custom-call | tf_op jit(solution)/shard_map/pallas_call | solution.py:265
  319.3 0.0 copy-start.2
  319.3 1.6 copy.15
  320.9 1.9 copy.21
  322.8 1.9 copy.22
  324.7 0.0 copy-done.2
  324.7 0.0 copy-start.1
  324.7 1.1 copy.23
  325.8 0.8 copy-done.1
  326.7 0.0 copy-start
  326.7 1.1 copy.24
  327.8 0.8 copy-done
  328.6 1.1 copy.25
Async XLA Ops:
  319.3 5.4 %copy-start.2 = (bf16[1024,768]{1,0:T(8,128)(2,1)S(1)}, bf16[1024,768]{1,0:T(8,128)(2,1)}, u32[]{:S(2)}) copy-start(bf16[1024,768]{1,0:T(8,128)(2,1)} %get-tuple-element.15) | copy-start | bytes 4718596
  324.7 2.0 copy-start.1
  326.7 2.0 copy-start
